TPU v7x, 256 devices: a whole 4x4x8 slice. The times are simulated.
256 devices in a mesh: pairs: 64 (over y, z, core), orb: 4 (over x).
Axes of the slice: x: 4, y: 4, z: 8, core: 2. Of those that a mesh axis runs over, the one named last changes fastest.
Arguments:
- amplitudes: float32 [1024, 128, 128], P(('pairs', 'orb')), may hold values from -4 to 4
- integrals: bfloat16 [1024, 128, 128], P(('pairs', 'orb')), may hold values from -6 to 6
- energies: float32 [1024, 128], P(('pairs', 'orb')), may hold values from 0.5 to 4
- intersections: bfloat16 [1024, 16, 128, 128], P(('pairs', 'orb')), may hold values from -0.5 to 0.5
- couplings: float32 [1024, 16], P(('pairs', 'orb')), may hold values from -2 to 2
- projector: float32 [1024, 128], P(('pairs', 'orb')), may hold values from -0.5 to 0.5
- pair_orbitals: int32 [1024, 2], P(('pairs', 'orb')), may hold values from 0 to 31
- coupled: int32 [1024, 16], replicated, may hold values from 0 to 1023, as said below
- pair_slot: int32 [1024], replicated, may hold values from 0 to 1023, as said below
Outputs:
- final_amplitudes: float32 [1024, 128, 128], P(('pairs', 'orb'))
- residual: float32 [1024, 128, 128], P(('pairs', 'orb'))
Inputs may be any that keep to these rules, and one draw needn't show every extreme that they name: `coupled`: each row holds 16 different pair ids, never the id of the pair held in that row's slot. The rows of one device name at most 1 different pairs held by the devices of any one pairs index, and exactly 1 held by the devices of the next pairs index. `pair_slot`: A permutation of the pair ids.
All inputs are finite; a program needn't handle non-finite values.
Results may differ from a plain program's by a relative error of at most 0.00037.
Values may be sent and summed in bfloat16 or wider, within the bound.
A program may use at most 64 MiB of HBM per device.

v0:
```python
import jax
import jax.numpy as jnp
from jax import lax
from jax.sharding import PartitionSpec as P

PAIRS_ORB = 32
ITERS = 2


def body(
    amplitudes,
    integrals,
    energies,
    intersections,
    couplings,
    projector,
    pair_orbitals,
    coupled,
    pair_slot,
):
    highest = lax.Precision.HIGHEST
    pair_count = lax.axis_size("pairs")
    orb_count = lax.axis_size("orb")
    devices = pair_count * orb_count
    per_device = amplitudes.shape[0]
    width = amplitudes.shape[1]
    total = coupled.shape[0]
    capacity = 1 + coupled.shape[1] // pair_count
    group = orb_count * per_device
    orbitals = total // PAIRS_ORB
    pair_idx = lax.axis_index("pairs")
    orb_idx = lax.axis_index("orb")
    device_id = pair_idx * orb_count + orb_idx
    targets = pair_slot[coupled]
    row_owner = jnp.broadcast_to(
        (jnp.arange(total, dtype=jnp.int32) // per_device)[:, None], targets.shape
    )
    needed = jnp.zeros((devices, total), jnp.int32).at[row_owner, targets].set(1)
    mine = lax.dynamic_slice_in_dim(needed, device_id, 1, 0)[0].reshape(pair_count, group)
    ranks = (jnp.cumsum(mine, axis=1) - 1).reshape(total)
    own_targets = lax.dynamic_slice_in_dim(targets, device_id * per_device, per_device, 0)
    slot_ids = jnp.arange(capacity, dtype=jnp.int32)
    group_cols = lax.dynamic_slice_in_dim(needed, pair_idx * group, group, 1)
    group_rank = jnp.cumsum(group_cols, axis=1) - 1
    entry_pos = own_targets // group * capacity + ranks[own_targets]
    dest_cols = group_cols.reshape(pair_count, orb_count, group)
    dest_cols = lax.dynamic_slice_in_dim(dest_cols, orb_idx, 1, 1)[:, 0]
    dest_rank = group_rank.reshape(pair_count, orb_count, group)
    dest_rank = lax.dynamic_slice_in_dim(dest_rank, orb_idx, 1, 1)[:, 0]
    select = (
        (dest_cols == 1)[:, None, :] & (dest_rank[:, None, :] == slot_ids[None, :, None])
    ).astype(jnp.bfloat16)
    orbital_ids = jnp.arange(orbitals, dtype=jnp.int32)
    first_hot = (pair_orbitals[:, 0:1] == orbital_ids[None, :]).astype(jnp.float32)
    second_hot = (pair_orbitals[:, 1:2] == orbital_ids[None, :]).astype(jnp.float32)
    denom = energies[:, :, None] + energies[:, None, :]
    state = amplitudes
    residual = amplitudes
    for step in range(ITERS):
        blocks = state.astype(jnp.bfloat16)
        group_blocks = lax.all_gather(blocks, "orb", axis=0, tiled=True)
        outgoing = jnp.einsum(
            "pcj,jxy->pcxy", select, group_blocks, preferred_element_type=jnp.float32
        )
        outgoing = outgoing.astype(jnp.bfloat16)
        arrived = lax.all_to_all(outgoing, "pairs", split_axis=0, concat_axis=0, tiled=True)
        arrived = arrived.reshape(pair_count * capacity, width, width)
        fetched = arrived[entry_pos]
        lifted = jnp.einsum(
            "pkab,pkbc->pkac", intersections, fetched, preferred_element_type=jnp.float32
        )
        scaled = (couplings[:, :, None, None] * lifted).astype(jnp.bfloat16)
        coupling = jnp.einsum(
            "pkac,pkdc->pad", scaled, intersections, preferred_element_type=jnp.float32
        )
        projected = jnp.einsum("pab,pb->pa", state, projector, precision=highest)
        partial_sum = jnp.dot(first_hot.T, projected, precision=highest) + jnp.dot(
            second_hot.T, projected, precision=highest
        )
        summed = lax.psum(partial_sum, ("pairs", "orb"))
        left = jnp.dot(first_hot, summed, precision=highest)
        right = jnp.dot(second_hot, summed, precision=highest)
        residual = (
            integrals.astype(jnp.float32)
            + energies[:, :, None] * state
            + state * energies[:, None, :]
            - coupling
            + left[:, :, None] * projector[:, None, :]
            + projector[:, :, None] * right[:, None, :]
        )
        state = state - residual / denom
    return (state, residual)


def solution(mesh):
    return jax.shard_map(
        body,
        mesh=mesh,
        in_specs=(
            P(("pairs", "orb"), None, None),
            P(("pairs", "orb"), None, None),
            P(("pairs", "orb"), None),
            P(("pairs", "orb"), None, None, None),
            P(("pairs", "orb"), None),
            P(("pairs", "orb"), None),
            P(("pairs", "orb"), None),
            P(),
            P(),
        ),
        out_specs=(P(("pairs", "orb"), None, None), P(("pairs", "orb"), None, None)),
        check_vma=False,
    )
```

profile of v0, /device:TPU:1, one launch (start us, length us, event | category | flops | bytes accessed | tf_op | source)
XLA Modules:
  0.0 392.0 jit_solution(17940552267861765877)
XLA Ops:
  0.6 0.0 copy-start
  0.7 0.6 add_select_fusion
  1.3 0.6 broadcast_compare_fusion
  1.9 0.8 compare_select_fusion.1
  2.7 0.2 copy.38
  2.9 0.2 reshape.137
  3.1 65.3 %gather_fusion = s32[16384]{0:T(1024)S(1)} fusion(s32[1024]{0:T(1024)S(1)} %copy-done.1, s32[16384]{0:T(1024)S(1)} %broadcast_clamp_fusion), kind=kCustom, calls=%fused_computation | custom fusion | bytes 196608 | tf_op jit(solution)/shard_map/gather | solution.py:34
  68.4 0.0 copy-start.3
  68.4 0.0 copy-start.4
  68.4 0.0 copy-start.9
  68.4 0.0 copy-start.8
  68.5 0.2 gather.15
  68.6 0.1 compare_select_fusion
  68.7 0.2 copy.39
  68.9 0.2 copy-done.3
  69.1 0.0 copy-done.4
  69.1 0.0 copy-done.6
  69.1 0.1 multiply_reduce_fusion
  69.2 0.1 and_reduce_fusion
  69.3 0.2 copy.40
  69.5 0.2 reshape.167
  69.7 0.0 copy-start.2
  69.8 0.6 broadcast.186
  70.4 60.8 %scatter_custom_fusion = s32[262144]{0:T(1024)S(1)} fusion(s32[16384]{0:T(1024)S(1)} %reshape.167, s32[16384]{0:T(1024)} %broadcast.186, s32[]{:T(128)} %constant.52.clone.1), kind=kCustom, calls=%fused_computation.28 | custom fusion | bytes 1049088
  131.2 1.1 reshape.134
  132.3 1.0 constant_dynamic-slice_fusion
  133.4 0.7 reduce_window_sum.22
  134.1 12.3 %all_gather.6 = bf16[16,128,128]{2,1,0:T(8,128)(2,1)S(1)} all-gather(bf16[4,128,128]{2,1,0:T(8,128)(2,1)S(1)} %convert_element_type.38), channel_id=1, replica_groups=mesh['pairs'=64,'orb'=4] {'orb'}, dimensions={0}, use_global_device_ids=true | all-gather | bytes 655360 | tf_op jit(solution)/shard_map/all_gather | solution.py:61
  146.4 0.7 convert_bitcast_fusion.1
  147.1 2.6 copy.45
  149.8 14.2 %all-to-all-start = ((bf16[64,1,128,128]{3,2,1,0:T(8,128)(2,1)}), bf16[64,1,128,128]{3,2,1,0:T(8,128)(2,1)}, u32[]{:S(2)}, u32[]{:S(2)}) async-start(bf16[64,1,128,128]{3,2,1,0:T(8,128)(2,1)} %copy.45), calls=%async_computation | async-start | bytes 4194304 | tf_op jit(solution)/shard_map/all_to_all | solution.py:66
  164.0 0.0 copy-start.7
  164.0 0.0 copy-start.5
  164.0 0.2 reshape.136
  164.2 0.8 dynamic-slice_reduce_fusion
  165.0 0.1 reshape_squeeze.3
  165.1 0.2 reduce_window_sum.23
  165.2 0.1 sub.37
  165.3 0.1 reshape.145
  165.4 0.7 gather_fusion.1
  166.2 0.1 reshape.144
  166.3 0.1 reshape.153
  166.4 0.5 fusion.65
  166.9 0.3 fusion.54
  167.2 0.3 convolution_add_fusion.1
  167.4 89.2 %psum.14 = f32[32,128]{1,0:T(8,128)S(1)} all-reduce(f32[32,128]{1,0:T(8,128)S(1)} %convolution_add_fusion.1), channel_id=1, replica_groups=mesh['pairs'=64,'orb'=4] {'pairs','orb'}, use_global_device_ids=true, to_apply=%region_3.4 | all-reduce | flops 4096 | bytes 32768 | tf_op jit(solution)/shard_map/psum | solution.py:80
  256.7 0.2 fusion.53
  256.9 0.2 fusion.50
  257.0 0.0 copy-start.11
  257.1 0.0 copy-start.12
  257.1 3.7 gather_fusion.2
  260.8 3.8 fusion.64
  264.6 11.4 %all_gather.7 = bf16[16,128,128]{2,1,0:T(8,128)(2,1)S(1)} all-gather(bf16[4,128,128]{2,1,0:T(8,128)(2,1)S(1)} %get-tuple-element.4), channel_id=1, replica_groups=mesh['pairs'=64,'orb'=4] {'orb'}, dimensions={0}, use_global_device_ids=true | all-gather | bytes 655360 | tf_op jit(solution)/shard_map/all_gather | solution.py:61
  276.1 0.7 convert_bitcast_fusion
  276.8 2.6 copy.50
  279.4 11.7 %all-to-all-start.1 = ((bf16[64,1,128,128]{3,2,1,0:T(8,128)(2,1)}), bf16[64,1,128,128]{3,2,1,0:T(8,128)(2,1)}, u32[]{:S(2)}, u32[]{:S(2)}) async-start(bf16[64,1,128,128]{3,2,1,0:T(8,128)(2,1)} %copy.50), calls=%async_computation.1 | async-start | bytes 4194304 | tf_op jit(solution)/shard_map/all_to_all | solution.py:66
  291.1 0.5 fusion.66
  291.6 0.3 fusion.52
  291.9 0.3 convolution_add_fusion
  292.2 91.1 %psum.15 = f32[32,128]{1,0:T(8,128)S(1)} all-reduce(f32[32,128]{1,0:T(8,128)S(1)} %convolution_add_fusion), channel_id=1, replica_groups=mesh['pairs'=64,'orb'=4] {'pairs','orb'}, use_global_device_ids=true, to_apply=%region_4.5 | all-reduce | flops 4096 | bytes 32768 | tf_op jit(solution)/shard_map/psum | solution.py:80
  383.3 0.2 fusion.51
  383.5 0.2 fusion.49
  383.7 3.7 gather_fusion.3
  387.4 4.6 %fusion.40 = (f32[4,128,128]{2,1,0:T(8,128)}, f32[4,128,128]{2,1,0:T(8,128)}) fusion(f32[4,128,128]{2,1,0:T(8,128)S(1)} %get-tuple-element.5, f32[4,128]{1,0:T(4,128)S(1)} %copy-done.12, f32[4,128]{1,0:T(4,128)S(1)} %fusion.49, f32[4,128]{1,0:T(4,128)S(1)} %copy-done.5, f32[4,128]{1,0:T(4,128)S(1)} %fusion.51, bf16[4,16,128,128]{3,2,1,0:T(8,128)(2,1)S(1)} %copy-done, ...), kind=kOutput, calls=%fused_computation.35 | convolution fusion | flops 539820032 | bytes 5120256 | tf_op jit(solution)/shard_map/pkac,pkdc->pad/dot_general | solution.py:73
  (27 shorter events, 0.2 us)
Async XLA Ops:
  0.6 260.2 %copy-start = (bf16[4,16,128,128]{3,2,1,0:T(8,128)(2,1)S(1)}, bf16[4,16,128,128]{3,2,1,0:T(8,128)(2,1)}, u32[]{:S(2)}) copy-start(bf16[4,16,128,128]{3,2,1,0:T(8,128)(2,1)} %param.12) | copy-start | bytes 6291460
  0.6 2.5 copy-start.1
  68.4 0.7 copy-start.3
  68.4 0.7 copy-start.4
  68.4 0.7 copy-start.6
  68.4 0.7 copy-start.9
  68.4 0.8 copy-start.8
  69.7 64.4 %copy-start.2 = (f32[4,128,128]{2,1,0:T(8,128)S(1)}, f32[4,128,128]{2,1,0:T(8,128)}, u32[]{:S(2)}) copy-start(f32[4,128,128]{2,1,0:T(8,128)} %param.9) | copy-start | bytes 786436
  149.8 107.3 %all-to-all-start = ((bf16[64,1,128,128]{3,2,1,0:T(8,128)(2,1)}), bf16[64,1,128,128]{3,2,1,0:T(8,128)(2,1)}, u32[]{:S(2)}, u32[]{:S(2)}) async-start(bf16[64,1,128,128]{3,2,1,0:T(8,128)(2,1)} %copy.45), calls=%async_computation | async-start | bytes 4194304 | tf_op jit(solution)/shard_map/all_to_all | solution.py:66
  164.0 2.4 copy-start.7
  164.0 2.4 copy-start.5
  257.0 3.8 copy-start.10
  257.0 3.8 copy-start.11
  257.1 3.8 copy-start.12
  279.4 104.3 %all-to-all-start.1 = ((bf16[64,1,128,128]{3,2,1,0:T(8,128)(2,1)}), bf16[64,1,128,128]{3,2,1,0:T(8,128)(2,1)}, u32[]{:S(2)}, u32[]{:S(2)}) async-start(bf16[64,1,128,128]{3,2,1,0:T(8,128)(2,1)} %copy.50), calls=%async_computation.1 | async-start | bytes 4194304 | tf_op jit(solution)/shard_map/all_to_all | solution.py:66
where the time goes:
time: 393 us; the launch traced here: 392 us
  blocking collectives  204 us (52%)
  local copies, waits for them, and re-layouts  145 us (37%)
  starting transfers between devices  25.9 us (7%)
  matrix products  12.6 us (3%)
    psum x2, blocking collectives, body(): summed = lax.psum(partial_sum, ('pairs', 'orb'))  180 us
    gather x3, local copies, waits for them, and re-layouts, body(): targets = pair_slot[coupled]  65.6 us
    unnamed x30, local copies, waits for them, and re-layouts  62.1 us
    all_to_all x2, starting transfers between devices, body(): lax.all_to_all(outgoing, 'pairs', split_axis=0, concat_axis=0, tiled=True)  25.9 us
    all_gather x2, blocking collectives, body(): group_blocks = lax.all_gather(blocks, 'orb', axis=0, tiled=True)  23.7 us
    dot_general x2, matrix products, body(): jnp.einsum('pkac,pkdc->pad', scaled, intersections, preferred_element_typ...  8.38 us
  transfers between devices with their start and end apart: 2, of which 0 were waited for; matrix products, arithmetic and copies ran while one was open for 1% of the time, Pallas kernels for 0%

commit v1 on v0

--- a/solution.py
+++ b/solution.py
@@ -77,7 +77,9 @@
         partial_sum = jnp.dot(first_hot.T, projected, precision=highest) + jnp.dot(
             second_hot.T, projected, precision=highest
         )
-        summed = lax.psum(partial_sum, ("pairs", "orb"))
+        summed = partial_sum
+        for b in ("pairs", "orb"):
+            summed = lax.psum(summed, b)
         left = jnp.dot(first_hot, summed, precision=highest)
         right = jnp.dot(second_hot, summed, precision=highest)
         residual = (

time: 393 us -> 807 us (2.05)
  blocking collectives: 204 us -> 606 us
    psum x2 -> x4, blocking collectives: 180 us -> 584 us  [body(): summed = lax.psum(summed, b)]
where the time goes in v1:
time: 807 us; the launch traced here: 799 us
  blocking collectives  606 us (75%)
  local copies, waits for them, and re-layouts  145 us (18%)
  starting transfers between devices  31.2 us (4%)
  matrix products  12.6 us (2%)
    psum x4, blocking collectives, body(): summed = lax.psum(summed, b)  584 us
    gather x3, local copies, waits for them, and re-layouts, body(): targets = pair_slot[coupled]  65.6 us
    unnamed x30, local copies, waits for them, and re-layouts  62.1 us
    all_to_all x2, starting transfers between devices, body(): lax.all_to_all(outgoing, 'pairs', split_axis=0, concat_axis=0, tiled=True)  31.2 us
    all_gather x2, blocking collectives, body(): group_blocks = lax.all_gather(blocks, 'orb', axis=0, tiled=True)  22.4 us
  transfers between devices with their start and end apart: 2, of which 0 were waited for; matrix products, arithmetic and copies ran while one was open for 1% of the time, Pallas kernels for 0%

profile of v1, /device:TPU:1, one launch (start us, length us, event | category | flops | bytes accessed | tf_op | source)
XLA Modules:
  0.0 799.4 jit_solution(15587189230968977783)
XLA Ops:
  0.6 0.0 copy-start
  0.7 0.6 add_select_fusion
  1.3 0.6 broadcast_compare_fusion
  1.9 0.8 compare_select_fusion.1
  2.7 0.2 copy.38
  2.9 0.2 reshape.137
  3.1 65.3 %gather_fusion = s32[16384]{0:T(1024)S(1)} fusion(s32[1024]{0:T(1024)S(1)} %copy-done.1, s32[16384]{0:T(1024)S(1)} %broadcast_clamp_fusion), kind=kCustom, calls=%fused_computation | custom fusion | bytes 196608 | tf_op jit(solution)/shard_map/gather | solution.py:34
  68.4 0.0 copy-start.3
  68.4 0.0 copy-start.9
  68.4 0.0 copy-start.8
  68.5 0.2 gather.15
  68.6 0.1 compare_select_fusion
  68.7 0.2 copy.39
  68.9 0.2 copy-done.3
  69.1 0.0 copy-done.4
  69.1 0.0 copy-done.6
  69.1 0.1 multiply_reduce_fusion
  69.2 0.1 and_reduce_fusion
  69.3 0.2 copy.40
  69.5 0.2 reshape.167
  69.7 0.0 copy-start.2
  69.8 0.6 broadcast.186
  70.4 60.8 %scatter_custom_fusion = s32[262144]{0:T(1024)S(1)} fusion(s32[16384]{0:T(1024)S(1)} %reshape.167, s32[16384]{0:T(1024)} %broadcast.186, s32[]{:T(128)} %constant.52.clone.1), kind=kCustom, calls=%fused_computation.28 | custom fusion | bytes 1049088
  131.2 1.1 reshape.134
  132.3 1.0 constant_dynamic-slice_fusion
  133.4 0.7 reduce_window_sum.22
  134.1 12.3 %all_gather.6 = bf16[16,128,128]{2,1,0:T(8,128)(2,1)S(1)} all-gather(bf16[4,128,128]{2,1,0:T(8,128)(2,1)S(1)} %convert_element_type.38), channel_id=1, replica_groups=mesh['pairs'=64,'orb'=4] {'orb'}, dimensions={0}, use_global_device_ids=true | all-gather | bytes 655360 | tf_op jit(solution)/shard_map/all_gather | solution.py:61
  146.4 0.7 convert_bitcast_fusion.1
  147.1 2.6 copy.45
  149.8 14.2 %all-to-all-start = ((bf16[64,1,128,128]{3,2,1,0:T(8,128)(2,1)}), bf16[64,1,128,128]{3,2,1,0:T(8,128)(2,1)}, u32[]{:S(2)}, u32[]{:S(2)}) async-start(bf16[64,1,128,128]{3,2,1,0:T(8,128)(2,1)} %copy.45), calls=%async_computation | async-start | bytes 4194304 | tf_op jit(solution)/shard_map/all_to_all | solution.py:66
  164.0 0.0 copy-start.7
  164.0 0.0 copy-start.5
  164.0 0.2 reshape.136
  164.2 0.8 dynamic-slice_reduce_fusion
  165.0 0.1 reshape_squeeze.3
  165.1 0.2 reduce_window_sum.23
  165.2 0.1 sub.37
  165.3 0.1 reshape.145
  165.4 0.7 gather_fusion.1
  166.2 0.1 reshape.144
  166.3 0.1 reshape.153
  166.4 0.5 fusion.65
  166.9 0.3 fusion.54
  167.2 0.3 convolution_add_fusion.1
  167.4 278.5 %psum.28 = f32[32,128]{1,0:T(8,128)S(1)} all-reduce(f32[32,128]{1,0:T(8,128)S(1)} %convolution_add_fusion.1), channel_id=1, replica_groups=mesh['pairs'=64,'orb'=4] {'pairs'}, use_global_device_ids=true, to_apply=%region_3.4 | all-reduce | flops 4096 | bytes 32768 | tf_op jit(solution)/shard_map/psum | solution.py:82
  445.9 13.6 %psum.29 = f32[32,128]{1,0:T(8,128)S(1)} all-reduce(f32[32,128]{1,0:T(8,128)S(1)} %psum.28), channel_id=1, replica_groups=mesh['pairs'=64,'orb'=4] {'orb'}, use_global_device_ids=true, to_apply=%region_4.5 | all-reduce | flops 4096 | bytes 32768 | tf_op jit(solution)/shard_map/psum | solution.py:82
  459.6 0.2 fusion.53
  459.7 0.2 fusion.50
  459.9 0.0 copy-start.11
  460.0 3.7 gather_fusion.2
  463.7 3.8 fusion.64
  467.5 10.1 %all_gather.7 = bf16[16,128,128]{2,1,0:T(8,128)(2,1)S(1)} all-gather(bf16[4,128,128]{2,1,0:T(8,128)(2,1)S(1)} %get-tuple-element.4), channel_id=1, replica_groups=mesh['pairs'=64,'orb'=4] {'orb'}, dimensions={0}, use_global_device_ids=true | all-gather | bytes 655360 | tf_op jit(solution)/shard_map/all_gather | solution.py:61
  477.6 0.7 convert_bitcast_fusion
  478.3 2.6 copy.50
  480.9 16.9 %all-to-all-start.1 = ((bf16[64,1,128,128]{3,2,1,0:T(8,128)(2,1)}), bf16[64,1,128,128]{3,2,1,0:T(8,128)(2,1)}, u32[]{:S(2)}, u32[]{:S(2)}) async-start(bf16[64,1,128,128]{3,2,1,0:T(8,128)(2,1)} %copy.50), calls=%async_computation.1 | async-start | bytes 4194304 | tf_op jit(solution)/shard_map/all_to_all | solution.py:66
  497.9 0.5 fusion.66
  498.4 0.3 fusion.52
  498.7 0.3 convolution_add_fusion
  499.0 280.9 %psum.30 = f32[32,128]{1,0:T(8,128)S(1)} all-reduce(f32[32,128]{1,0:T(8,128)S(1)} %convolution_add_fusion), channel_id=1, replica_groups=mesh['pairs'=64,'orb'=4] {'pairs'}, use_global_device_ids=true, to_apply=%region_5.6 | all-reduce | flops 4096 | bytes 32768 | tf_op jit(solution)/shard_map/psum | solution.py:82
  779.9 10.8 %psum.31 = f32[32,128]{1,0:T(8,128)S(1)} all-reduce(f32[32,128]{1,0:T(8,128)S(1)} %psum.30), channel_id=1, replica_groups=mesh['pairs'=64,'orb'=4] {'orb'}, use_global_device_ids=true, to_apply=%region_6.7 | all-reduce | flops 4096 | bytes 32768 | tf_op jit(solution)/shard_map/psum | solution.py:82
  790.7 0.2 fusion.51
  790.9 0.2 fusion.49
  791.1 3.7 gather_fusion.3
  794.8 4.6 fusion.40
  (29 shorter events, 0.2 us)
Async XLA Ops:
  0.6 463.1 %copy-start = (bf16[4,16,128,128]{3,2,1,0:T(8,128)(2,1)S(1)}, bf16[4,16,128,128]{3,2,1,0:T(8,128)(2,1)}, u32[]{:S(2)}) copy-start(bf16[4,16,128,128]{3,2,1,0:T(8,128)(2,1)} %param.12) | copy-start | bytes 6291460
  0.6 2.5 copy-start.1
  68.4 0.7 copy-start.3
  68.4 0.7 copy-start.4
  68.4 0.7 copy-start.6
  68.4 0.7 copy-start.9
  68.4 0.8 copy-start.8
  69.7 64.4 %copy-start.2 = (f32[4,128,128]{2,1,0:T(8,128)S(1)}, f32[4,128,128]{2,1,0:T(8,128)}, u32[]{:S(2)}) copy-start(f32[4,128,128]{2,1,0:T(8,128)} %param.9) | copy-start | bytes 786436
  149.8 310.2 %all-to-all-start = ((bf16[64,1,128,128]{3,2,1,0:T(8,128)(2,1)}), bf16[64,1,128,128]{3,2,1,0:T(8,128)(2,1)}, u32[]{:S(2)}, u32[]{:S(2)}) async-start(bf16[64,1,128,128]{3,2,1,0:T(8,128)(2,1)} %copy.45), calls=%async_computation | async-start | bytes 4194304 | tf_op jit(solution)/shard_map/all_to_all | solution.py:66
  164.0 2.4 copy-start.7
  164.0 2.4 copy-start.5
  459.9 3.8 copy-start.10
  459.9 3.8 copy-start.11
  459.9 3.8 copy-start.12
  480.9 310.1 %all-to-all-start.1 = ((bf16[64,1,128,128]{3,2,1,0:T(8,128)(2,1)}), bf16[64,1,128,128]{3,2,1,0:T(8,128)(2,1)}, u32[]{:S(2)}, u32[]{:S(2)}) async-start(bf16[64,1,128,128]{3,2,1,0:T(8,128)(2,1)} %copy.50), calls=%async_computation.1 | async-start | bytes 4194304 | tf_op jit(solution)/shard_map/all_to_all | solution.py:66
